TPU v7x, 32 devices: a whole 2x2x4 slice. The times are simulated.
32 devices in a mesh: sib: 2 (over core), row: 4 (over z), col: 4 (over y, x).
Axes of the slice: x: 2, y: 2, z: 4, core: 2. Of those that a mesh axis runs over, the one named last changes fastest.
Arguments:
- child_front: float32 [2, 2048, 2048], P('sib', 'row', 'col'), may hold values from -6 to 6
- child_panel: float32 [2, 2048, 1024], P('sib', ('row', 'col')), may hold values from -0.42 to 0.42
- block_map: int32 [2, 16], replicated, may hold values from 0 to 23, as said below
- parent_front: float32 [3072, 3072], P(('row', 'sib'), 'col'), may hold values from -6 to 6
- pivot_inverse: float32 [512, 512], replicated, may hold values from -0.03 to 0.1, as said below
Outputs:
- parent_out: float32 [3072, 3072], P(('row', 'sib'), 'col')
Inputs may be any that keep to these rules, and one draw needn't show every extreme that they name: `block_map`: each row is strictly increasing. A child block i that lands in parent block g * 6 + k with 0 <= k < 6 satisfies g * 4 - 2 <= i < (g + 1) * 4; the lower end is met for g = 1 in every draw, and the last parent block is always named. `pivot_inverse`: lower triangular with diagonal entries from 0.05 to 0.1.
All inputs are finite; a program needn't handle non-finite values.
Results may differ from a plain program's by a relative error of at most 0.0001.
Values sent between devices are 32-bit elements; how exact they have to be, the bound alone decides.
No kernel may reach another device: no remote copies, remote signals or barrier semaphores. Data moves between devices by JAX's collectives and lax.ppermute only.
A program may use at most 64 MiB of HBM per device.

v0:
```python
import jax
import jax.numpy as jnp
from jax import lax
from jax.sharding import PartitionSpec as P

BLK = 128
CBD = 4
PBD = 6
HB = 2
PANEL = 512


def from_root(value, axis, source):
    kept = jnp.where(lax.axis_index(axis) == source, value, 0).astype(value.dtype)
    return lax.psum(kept, axis)


def shifted(value, axis, steps):
    count = lax.axis_size(axis)
    initial, last = (max(0, -steps), min(count, count - steps))
    return lax.ppermute(value, axis, [(source, source + steps) for source in range(initial, last)])


def choose_blocks(block_row, device, child_span, parent_span, edge_span):
    padded = jnp.concatenate([jnp.full((edge_span,), -1, jnp.int32), block_row])
    window = lax.dynamic_slice_in_dim(padded, device * child_span, child_span + edge_span)
    target = device * parent_span + jnp.arange(parent_span, dtype=jnp.int32)
    return (window[None, :] == target[:, None]).astype(jnp.float32)


def times_inverse(rows_part, pivot_inverse):
    return lax.dot_general(
        rows_part,
        pivot_inverse,
        (((1,), (1,)), ((), ())),
        precision=lax.Precision.HIGHEST,
        preferred_element_type=jnp.float32,
    )


def shards(child_front, child_panel, block_map, parent_front, pivot_inverse):
    front_index = lax.axis_index("sib")
    row_index = lax.axis_index("row")
    col_index = lax.axis_index("col")
    child_rows = child_front.shape[1]
    parent_rows = parent_front.shape[0]
    parent_cols = parent_front.shape[1]
    edge_width = HB * BLK
    span_blocks = CBD + HB
    rows_local = lax.all_gather(child_panel, "col", axis=1, tiled=True)[0]
    cols_local = from_root(rows_local, "row", col_index)
    update = child_front[0] - lax.dot_general(
        rows_local,
        cols_local,
        (((1,), (1,)), ((), ())),
        precision=lax.Precision.HIGHEST,
        preferred_element_type=jnp.float32,
    )
    my_map = lax.dynamic_index_in_dim(block_map, front_index, 0, keepdims=False)
    left_cols = shifted(update[:, -edge_width:], "col", 1)
    col_window = jnp.concatenate([left_cols, update], axis=1).reshape(child_rows, span_blocks, BLK)
    col_pick = choose_blocks(my_map, col_index, CBD, PBD, HB)
    spread_cols = jnp.einsum(
        "rwk,qw->rqk", col_window, col_pick, precision=lax.Precision.HIGHEST
    ).reshape(child_rows, PBD * BLK)
    left_rows = shifted(spread_cols[-edge_width:], "row", 1)
    row_window = jnp.concatenate([left_rows, spread_cols], axis=0).reshape(
        span_blocks, BLK, PBD * BLK
    )
    row_pick = choose_blocks(my_map, row_index, CBD, PBD, HB)
    spread_both = jnp.einsum(
        "wtc,qw->qtc", row_window, row_pick, precision=lax.Precision.HIGHEST
    ).reshape(PBD * BLK, PBD * BLK)
    summed = lax.psum_scatter(spread_both, "sib", scatter_dimension=0, tiled=True)
    assembled = parent_front + summed
    local_factor = times_inverse(assembled[:, :PANEL], pivot_inverse)
    factor_rows = from_root(local_factor, "col", 0)
    owner_rows = from_root(factor_rows, "row", col_index)
    col_factor = lax.all_gather(owner_rows, "sib", axis=0, tiled=True)
    product = lax.dot_general(
        factor_rows,
        col_factor,
        (((1,), (1,)), ((), ())),
        precision=lax.Precision.HIGHEST,
        preferred_element_type=jnp.float32,
    )
    global_rows = (row_index * 2 + front_index) * parent_rows + jnp.arange(
        parent_rows, dtype=jnp.int32
    )
    global_cols = col_index * parent_cols + jnp.arange(parent_cols, dtype=jnp.int32)
    inside = (global_rows[:, None] >= PANEL) & (global_cols[None, :] >= PANEL)
    trailing = jnp.where(inside, assembled - product, assembled)
    factor_wide = jnp.pad(factor_rows, ((0, 0), (0, parent_cols - PANEL)))
    return jnp.where(global_cols[None, :] < PANEL, factor_wide, trailing)


def solution(mesh):
    in_specs = (
        P("sib", "row", "col"),
        P("sib", ("row", "col"), None),
        P(),
        P(("row", "sib"), "col"),
        P(),
    )
    out_specs = P(("row", "sib"), "col")
    return jax.shard_map(shards, mesh=mesh, in_specs=in_specs, out_specs=out_specs, check_vma=False)
```

profile of v0, /device:TPU:0, one launch (start us, length us, event | category | flops | bytes accessed | tf_op | source)
XLA Modules:
  0.0 330.3 jit_solution(467878976344165727)
XLA Ops:
  7.3 39.8 %all-gather.3.cloned.1.call-done = f32[1,512,1024]{2,1,0:T(8,128)} async-done(((f32[1,128,1024]{2,1,0:T(8,128)}), f32[1,512,1024]{2,1,0:T(8,128)}) %all-gather.3.cloned.1.call-update) | async-done | bytes 2097168 | tf_op jit(solution)/shard_map/all_gather | solution.py:50
  47.1 3.2 bitcast_select_fusion
  50.4 2.7 copy.8
  53.1 83.6 %all-reduce.6.cloned.1.call-done = f32[512,1024]{1,0:T(8,128)} async-done(((f32[512,1024]{1,0:T(8,128)}), f32[512,1024]{1,0:T(8,128)}) %all-reduce.6.cloned.1.call-update) | async-done | bytes 2097168 | tf_op jit(solution)/shard_map/psum | solution.py:15
  136.7 5.4 %fusion.8 = f32[512,512]{0,1:T(8,128)S(1)} fusion(f32[512,1024]{1,0:T(8,128)} %all-reduce.6.cloned.1.call-done, f32[1,512,1024]{2,1,0:T(8,128)S(1)} %copy-done.1, f32[1,512,512]{1,2,0:T(8,128)} %copy.8), kind=kOutput, calls=%fused_computation.11 | convolution fusion | flops 3221487616 | bytes 6291456 | tf_op jit(solution)/shard_map/dot_general | solution.py:52
  143.1 3.4 %collective-permute-start = (f32[512,256]{0,1:T(8,128)S(1)}, f32[512,256]{0,1:T(8,128)S(1)}, u32[]{:S(2)}, u32[]{:S(2)}) collective-permute-start(f32[512,256]{0,1:T(8,128)S(1)} %slice.16), channel_id=1, source_target_pairs={{0,1},{1,2},{2,3},{4,5},{5,6},{6,7},{8,9},{9,10},{10,11},{12,13},{... | collective-permute-start | bytes 1572872 | tf_op jit(solution)/shard_map/ppermute | solution.py:21
  146.7 10.7 %collective-permute-done = f32[512,256]{0,1:T(8,128)S(1)} collective-permute-done((f32[512,256]{0,1:T(8,128)S(1)}, f32[512,256]{0,1:T(8,128)S(1)}, u32[]{:S(2)}, u32[]{:S(2)}) %collective-permute-start) | collective-permute-done | bytes 524320 | tf_op jit(solution)/shard_map/ppermute | solution.py:21
  158.7 1.8 copy.9
  160.5 2.7 convolution_bitcast_fusion
  164.2 2.4 copy.10
  166.6 3.0 collective-permute-start.1
  169.6 1.7 copy.11
  171.3 13.2 %collective-permute-done.1 = f32[256,768]{0,1:T(8,128)} collective-permute-done((f32[256,768]{0,1:T(8,128)}, f32[256,768]{0,1:T(8,128)}, u32[]{:S(2)}, u32[]{:S(2)}) %collective-permute-start.1) | collective-permute-done | bytes 786464 | tf_op jit(solution)/shard_map/ppermute | solution.py:21
  184.5 3.2 pad_maximum_fusion
  187.7 2.0 copy.12
  189.7 2.9 fusion
  192.6 2.2 copy.14
  195.0 13.4 %reduce-scatter.2.cloned.1.call-done = f32[384,768]{1,0:T(8,128)} async-done(((f32[768,768]{1,0:T(8,128)}), f32[384,768]{1,0:T(8,128)}) %reduce-scatter.2.cloned.1.call-update) | async-done | bytes 1179664 | tf_op jit(solution)/shard_map/reduce_scatter | solution.py:74
  209.8 2.3 convolution_select_fusion
  212.2 50.0 %all-reduce.8.cloned.1.call-done = f32[384,512]{1,0:T(8,128)} async-done(((f32[384,512]{1,0:T(8,128)}), f32[384,512]{1,0:T(8,128)}) %all-reduce.8.cloned.1.call-update) | async-done | bytes 786448 | tf_op jit(solution)/shard_map/psum | solution.py:15
  262.2 2.1 broadcast_select_fusion
  264.5 44.0 %all-reduce.10.cloned.1.call-done = f32[384,512]{1,0:T(8,128)} async-done(((f32[384,512]{1,0:T(8,128)}), f32[384,512]{1,0:T(8,128)}) %all-reduce.10.cloned.1.call-update) | async-done | bytes 786448 | tf_op jit(solution)/shard_map/psum | solution.py:15
  308.5 10.4 %all-gather.5.cloned.1.call-done = f32[768,512]{1,0:T(8,128)} async-done(((f32[384,512]{1,0:T(8,128)}), f32[768,512]{1,0:T(8,128)}) %all-gather.5.cloned.1.call-update) | async-done | bytes 1572880 | tf_op jit(solution)/shard_map/all_gather | solution.py:79
  318.9 4.6 %fusion.4 = f32[384,768]{1,0:T(8,128)} fusion(f32[384,768]{1,0:T(8,128)S(1)} %add.80, f32[384,512]{1,0:T(8,128)S(1)} %copy-done.3, f32[768,512]{1,0:T(8,128)} %all-gather.5.cloned.1.call-done, pred[768]{0:T(1024)(128)(4,1)S(1)} %get-tuple-element.7, pred[768]{0:T(1024)(128)(4,1)S(1)} %get-tuple-element.8, pred[384]{0:T(512)(128)(4,1)S(1)} %add_compare_fusion), kind=kOutput, calls=%fused_computation.9 | convolution fusion | flops 1813118976 | bytes 4720512 | tf_op jit(solution)/shard_map/dot_general | solution.py:80
  (34 shorter events, 6.1 us)
Async XLA Ops:
  6.5 203.3 %copy-start = (f32[512,512]{1,0:T(8,128)S(1)}, f32[512,512]{1,0:T(8,128)}, u32[]{:S(2)}) copy-start(f32[512,512]{1,0:T(8,128)} %param.9) | copy-start | bytes 3145732
  6.5 40.6 %all-gather.3.cloned.1.call-start = ((), (), s32[]{:S(2)}) async-start(), calls=%async_computation.1 | async-start | bytes 2621440 | tf_op jit(solution)/shard_map/all_gather | solution.py:50
  7.3 129.4 %all-reduce.6.cloned.1.call-start = ((), (), s32[]{:S(2)}) async-start(), calls=%async_computation.2 | async-start | bytes 4194304 | tf_op jit(solution)/shard_map/psum | solution.py:15
  50.3 86.3 %copy-start.1 = (f32[1,512,1024]{2,1,0:T(8,128)S(1)}, f32[1,512,1024]{2,1,0:T(8,128)}, u32[]{:S(2)}) copy-start(f32[1,512,1024]{2,1,0:T(8,128)} %all-gather.3.cloned.1.call-done) | copy-start | bytes 6291460
  50.4 158.0 %reduce-scatter.2.cloned.1.call-start = ((), (), s32[]{:S(2)}) async-start(), calls=%async_computation.3 | async-start | bytes 3538944 | tf_op jit(solution)/shard_map/reduce_scatter | solution.py:74
  53.1 93.4 %copy-start.5 = (s32[2,16]{1,0:T(2,128)S(1)}, s32[2,16]{1,0:T(2,128)}, u32[]{:S(2)}) copy-start(s32[2,16]{1,0:T(2,128)} %param.7) | copy-start | bytes 388
  142.1 1.0 copy-start.2
  143.1 14.2 %collective-permute-start = (f32[512,256]{0,1:T(8,128)S(1)}, f32[512,256]{0,1:T(8,128)S(1)}, u32[]{:S(2)}, u32[]{:S(2)}) collective-permute-start(f32[512,256]{0,1:T(8,128)S(1)} %slice.16), channel_id=1, source_target_pairs={{0,1},{1,2},{2,3},{4,5},{5,6},{6,7},{8,9},{9,10},{10,11},{12,13},{... | collective-permute-start | bytes 1572872 | tf_op jit(solution)/shard_map/ppermute | solution.py:21
  166.6 17.9 %collective-permute-start.1 = (f32[256,768]{0,1:T(8,128)}, f32[256,768]{0,1:T(8,128)}, u32[]{:S(2)}, u32[]{:S(2)}) collective-permute-start(f32[256,768]{0,1:T(8,128)} %bitcast.38), channel_id=1, source_target_pairs={{0,4},{4,8},{8,12},{1,5},{5,9},{9,13},{2,6},{6,10},{10,14},{3,7},{... | collective-permute-start | bytes 2359304 | tf_op jit(solution)/shard_map/ppermute | solution.py:21
  194.8 13.6 %copy-start.4 = (f32[384,768]{1,0:T(8,128)S(1)}, f32[384,768]{1,0:T(8,128)}, u32[]{:S(2)}) copy-start(f32[384,768]{1,0:T(8,128)} %param.8) | copy-start | bytes 3538948
  194.8 67.4 %all-reduce.8.cloned.1.call-start = ((), (), s32[]{:S(2)}) async-start(), calls=%async_computation.4 | async-start | bytes 1572864 | tf_op jit(solution)/shard_map/psum | solution.py:15
  212.2 96.2 %all-reduce.10.cloned.1.call-start = ((), (), s32[]{:S(2)}) async-start(), calls=%async_computation.5 | async-start | bytes 1572864 | tf_op jit(solution)/shard_map/psum | solution.py:15
  262.2 56.7 %copy-start.3 = (f32[384,512]{1,0:T(8,128)S(1)}, f32[384,512]{1,0:T(8,128)}, u32[]{:S(2)}) copy-start(f32[384,512]{1,0:T(8,128)} %all-reduce.8.cloned.1.call-done) | copy-start | bytes 2359300
  264.4 54.5 %all-gather.5.cloned.1.call-start = ((), (), s32[]{:S(2)}) async-start(), calls=%async_computation.6 | async-start | bytes 2359296 | tf_op jit(solution)/shard_map/all_gather | solution.py:79
Sparse Core Ops, SparseCore 0:
  9.2 37.8 all-gather.2
  50.5 86.1 all-reduce.5
  194.9 13.4 reduce-scatter.1
  212.3 49.8 all-reduce.7
  264.5 43.8 all-reduce.9
  309.8 9.0 all-gather.4
where the time goes:
time: 331 us; the launch traced here: 330 us
  waiting for transfers between devices  266 us (80%)
  matrix products  17.9 us (5%)
  local copies, waits for them, and re-layouts  14.9 us (5%)
  between operations  13.6 us (4%)
  other arithmetic  11.4 us (3%)
  starting transfers between devices  6.82 us (2%)
    psum x3, waiting for transfers between devices, from_root(): return lax.psum(kept, axis)  178 us
    all_gather x1, waiting for transfers between devices, shards(): rows_local = lax.all_gather(child_panel, 'col', axis=1, tiled=True)[0]  39.8 us
    ppermute x2, waiting for transfers between devices, shifted(): lax.ppermute(value, axis, [(source, source + steps) for source in range(i...  23.8 us
    reduce_scatter x1, waiting for transfers between devices, shards(): lax.psum_scatter(spread_both, 'sib', scatter_dimension=0, tiled=True)  13.4 us
    all_gather x1, waiting for transfers between devices, shards(): col_factor = lax.all_gather(owner_rows, 'sib', axis=0, tiled=True)  10.4 us
  transfers between devices with their start and end apart: 8, of which 8 were waited for; matrix products, arithmetic and copies ran while one was open for 1% of the time, Pallas kernels for 0%

commit v1 on v0

--- a/solution.py
+++ b/solution.py
@@ -47,7 +47,9 @@
     parent_cols = parent_front.shape[1]
     edge_width = HB * BLK
     span_blocks = CBD + HB
-    rows_local = lax.all_gather(child_panel, "col", axis=1, tiled=True)[0]
+    rows_local = jnp.concatenate(
+        lax.all_to_all(jnp.stack([child_panel] * lax.axis_size("col")), "col", 0, 0), axis=1
+    )[0]
     cols_local = from_root(rows_local, "row", col_index)
     update = child_front[0] - lax.dot_general(
         rows_local,

time: 331 us -> 321 us (0.970)
  waiting for transfers between devices: 266 us -> 251 us
  starting transfers between devices: 6.82 us -> 12 us
    all_gather x1 -> x0, waiting for transfers between devices: 39.8 us -> none  [shards(): rows_local = lax.all_gather(child_panel, 'col', axis=1, tiled=True)[0]]
    all_to_all x0 -> x1, waiting for transfers between devices: none -> 24.9 us  [shards(): lax.all_to_all(jnp.stack([child_panel] * lax.axis_size('col')), 'col', 0, 0)]
    all_to_all x0 -> x1, starting transfers between devices: none -> 5.19 us  [shards(): lax.all_to_all(jnp.stack([child_panel] * lax.axis_size('col')), 'col', 0, 0)]
where the time goes in v1:
time: 321 us
  waiting for transfers between devices  251 us (78%)
  matrix products  17.9 us (6%)
  local copies, waits for them, and re-layouts  17.5 us (5%)
  between operations  13.3 us (4%)
  starting transfers between devices  12 us (4%)
  other arithmetic  9.63 us (3%)
    psum x3, waiting for transfers between devices, from_root(): return lax.psum(kept, axis)  178 us
    all_to_all x1, waiting for transfers between devices, shards(): lax.all_to_all(jnp.stack([child_panel] * lax.axis_size('col')), 'col', 0, 0)  24.9 us
    ppermute x2, waiting for transfers between devices, shifted(): lax.ppermute(value, axis, [(source, source + steps) for source in range(i...  23.9 us
    reduce_scatter x1, waiting for transfers between devices, shards(): lax.psum_scatter(spread_both, 'sib', scatter_dimension=0, tiled=True)  13.3 us
    all_gather x1, waiting for transfers between devices, shards(): col_factor = lax.all_gather(owner_rows, 'sib', axis=0, tiled=True)  10.4 us
    ppermute x2, starting transfers between devices, shifted(): lax.ppermute(value, axis, [(source, source + steps) for source in range(i...  6.42 us
  transfers between devices with their start and end apart: 8, of which 8 were waited for; matrix products, arithmetic and copies ran while one was open for 1% of the time, Pallas kernels for 0%

profile of v1, /device:TPU:0, one launch (start us, length us, event | category | flops | bytes accessed | tf_op | source)
XLA Modules:
  0.0 320.9 jit_solution(10532591044226627049)
XLA Ops:
  6.5 2.7 stack.2
  9.3 5.2 %all-to-all-start = ((f32[4,1,128,1024]{3,2,1,0:T(8,128)}), f32[4,1,128,1024]{3,2,1,0:T(8,128)S(1)}, u32[]{:S(2)}, u32[]{:S(2)}) async-start(f32[4,1,128,1024]{3,2,1,0:T(8,128)} %stack.2), calls=%async_computation | async-start | bytes 4194304 | tf_op jit(solution)/shard_map/all_to_all | solution.py:51
  14.5 24.9 %all-to-all-done = f32[4,1,128,1024]{3,2,1,0:T(8,128)S(1)} async-done(((f32[4,1,128,1024]{3,2,1,0:T(8,128)}), f32[4,1,128,1024]{3,2,1,0:T(8,128)S(1)}, u32[]{:S(2)}, u32[]{:S(2)}) %all-to-all-start) | async-done | bytes 2097184 | tf_op jit(solution)/shard_map/all_to_all | solution.py:51
  40.9 2.5 copy.15
  43.4 84.1 %all-reduce.6.cloned.1.call-done = f32[512,1024]{1,0:T(8,128)} async-done(((f32[512,1024]{1,0:T(8,128)}), f32[512,1024]{1,0:T(8,128)}) %all-reduce.6.cloned.1.call-update) | async-done | bytes 2097168 | tf_op jit(solution)/shard_map/psum | solution.py:15
  127.6 5.4 %fusion.3 = f32[512,512]{0,1:T(8,128)S(1)} fusion(f32[512,1024]{1,0:T(8,128)} %all-reduce.6.cloned.1.call-done, f32[512,1024]{1,0:T(8,128)S(1)} %bitcast.30, f32[1,512,512]{1,2,0:T(8,128)} %copy.15), kind=kOutput, calls=%fused_computation.8 | convolution fusion | flops 3221487616 | bytes 6291456 | tf_op jit(solution)/shard_map/dot_general | solution.py:54
  134.0 3.4 %collective-permute-start = (f32[512,256]{0,1:T(8,128)S(1)}, f32[512,256]{0,1:T(8,128)S(1)}, u32[]{:S(2)}, u32[]{:S(2)}) collective-permute-start(f32[512,256]{0,1:T(8,128)S(1)} %slice.16), channel_id=1, source_target_pairs={{0,1},{1,2},{2,3},{4,5},{5,6},{6,7},{8,9},{9,10},{10,11},{12,13},{... | collective-permute-start | bytes 1572872 | tf_op jit(solution)/shard_map/ppermute | solution.py:21
  137.6 10.7 %collective-permute-done = f32[512,256]{0,1:T(8,128)S(1)} collective-permute-done((f32[512,256]{0,1:T(8,128)S(1)}, f32[512,256]{0,1:T(8,128)S(1)}, u32[]{:S(2)}, u32[]{:S(2)}) %collective-permute-start) | collective-permute-done | bytes 524320 | tf_op jit(solution)/shard_map/ppermute | solution.py:21
  149.6 1.8 copy.16
  151.4 2.7 convolution_bitcast_fusion
  155.1 2.4 copy.17
  157.5 3.0 collective-permute-start.1
  162.2 13.2 %collective-permute-done.1 = f32[256,768]{0,1:T(8,128)} collective-permute-done((f32[256,768]{0,1:T(8,128)}, f32[256,768]{0,1:T(8,128)}, u32[]{:S(2)}, u32[]{:S(2)}) %collective-permute-start.1) | collective-permute-done | bytes 786464 | tf_op jit(solution)/shard_map/ppermute | solution.py:21
  175.4 3.2 pad_maximum_fusion
  178.6 2.0 copy.19
  180.6 2.9 fusion
  183.5 2.2 copy.21
  185.9 13.3 %reduce-scatter.2.cloned.1.call-done = f32[384,768]{1,0:T(8,128)} async-done(((f32[768,768]{1,0:T(8,128)}), f32[384,768]{1,0:T(8,128)}) %reduce-scatter.2.cloned.1.call-update) | async-done | bytes 1179664 | tf_op jit(solution)/shard_map/reduce_scatter | solution.py:76
  200.7 2.3 convolution_select_fusion
  203.1 50.0 %all-reduce.8.cloned.1.call-done = f32[384,512]{1,0:T(8,128)} async-done(((f32[384,512]{1,0:T(8,128)}), f32[384,512]{1,0:T(8,128)}) %all-reduce.8.cloned.1.call-update) | async-done | bytes 786448 | tf_op jit(solution)/shard_map/psum | solution.py:15
  253.1 2.1 broadcast_select_fusion.1
  255.4 44.0 %all-reduce.10.cloned.1.call-done = f32[384,512]{1,0:T(8,128)} async-done(((f32[384,512]{1,0:T(8,128)}), f32[384,512]{1,0:T(8,128)}) %all-reduce.10.cloned.1.call-update) | async-done | bytes 786448 | tf_op jit(solution)/shard_map/psum | solution.py:15
  299.4 10.4 %all-gather.2.cloned.1.call-done = f32[768,512]{1,0:T(8,128)} async-done(((f32[384,512]{1,0:T(8,128)}), f32[768,512]{1,0:T(8,128)}) %all-gather.2.cloned.1.call-update) | async-done | bytes 1572880 | tf_op jit(solution)/shard_map/all_gather | solution.py:81
  309.8 4.6 %fusion.2 = f32[384,768]{1,0:T(8,128)} fusion(f32[384,768]{1,0:T(8,128)S(1)} %add.80, f32[384,512]{1,0:T(8,128)S(1)} %copy-done.2, f32[768,512]{1,0:T(8,128)} %all-gather.2.cloned.1.call-done, pred[768]{0:T(1024)(128)(4,1)S(1)} %get-tuple-element.7, pred[768]{0:T(1024)(128)(4,1)S(1)} %get-tuple-element.8, pred[384]{0:T(512)(128)(4,1)S(1)} %add_compare_fusion), kind=kOutput, calls=%fused_computation.6 | convolution fusion | flops 1813118976 | bytes 4720512 | tf_op jit(solution)/shard_map/dot_general | solution.py:82
  (32 shorter events, 8.5 us)
Async XLA Ops:
  6.5 194.2 %copy-start = (f32[512,512]{1,0:T(8,128)S(1)}, f32[512,512]{1,0:T(8,128)}, u32[]{:S(2)}) copy-start(f32[512,512]{1,0:T(8,128)} %param.9) | copy-start | bytes 3145732
  9.3 30.1 %all-to-all-start = ((f32[4,1,128,1024]{3,2,1,0:T(8,128)}), f32[4,1,128,1024]{3,2,1,0:T(8,128)S(1)}, u32[]{:S(2)}, u32[]{:S(2)}) async-start(f32[4,1,128,1024]{3,2,1,0:T(8,128)} %stack.2), calls=%async_computation | async-start | bytes 4194304 | tf_op jit(solution)/shard_map/all_to_all | solution.py:51
  14.5 113.1 %all-reduce.6.cloned.1.call-start = ((), (), s32[]{:S(2)}) async-start(), calls=%async_computation.2 | async-start | bytes 4194304 | tf_op jit(solution)/shard_map/psum | solution.py:15
  40.9 158.4 %reduce-scatter.2.cloned.1.call-start = ((), (), s32[]{:S(2)}) async-start(), calls=%async_computation.3 | async-start | bytes 3538944 | tf_op jit(solution)/shard_map/reduce_scatter | solution.py:76
  127.6 9.9 %copy-start.4 = (s32[2,16]{1,0:T(2,128)S(1)}, s32[2,16]{1,0:T(2,128)}, u32[]{:S(2)}) copy-start(s32[2,16]{1,0:T(2,128)} %param.7) | copy-start | bytes 388
  133.0 1.0 copy-start.1
  134.0 14.2 %collective-permute-start = (f32[512,256]{0,1:T(8,128)S(1)}, f32[512,256]{0,1:T(8,128)S(1)}, u32[]{:S(2)}, u32[]{:S(2)}) collective-permute-start(f32[512,256]{0,1:T(8,128)S(1)} %slice.16), channel_id=1, source_target_pairs={{0,1},{1,2},{2,3},{4,5},{5,6},{6,7},{8,9},{9,10},{10,11},{12,13},{... | collective-permute-start | bytes 1572872 | tf_op jit(solution)/shard_map/ppermute | solution.py:21
  157.5 17.9 %collective-permute-start.1 = (f32[256,768]{0,1:T(8,128)}, f32[256,768]{0,1:T(8,128)}, u32[]{:S(2)}, u32[]{:S(2)}) collective-permute-start(f32[256,768]{0,1:T(8,128)} %bitcast.35), channel_id=1, source_target_pairs={{0,4},{4,8},{8,12},{1,5},{5,9},{9,13},{2,6},{6,10},{10,14},{3,7},{... | collective-permute-start | bytes 2359304 | tf_op jit(solution)/shard_map/ppermute | solution.py:21
  185.7 13.6 %copy-start.3 = (f32[384,768]{1,0:T(8,128)S(1)}, f32[384,768]{1,0:T(8,128)}, u32[]{:S(2)}) copy-start(f32[384,768]{1,0:T(8,128)} %param.8) | copy-start | bytes 3538948
  185.7 67.4 %all-reduce.8.cloned.1.call-start = ((), (), s32[]{:S(2)}) async-start(), calls=%async_computation.4 | async-start | bytes 1572864 | tf_op jit(solution)/shard_map/psum | solution.py:15
  203.1 96.3 %all-reduce.10.cloned.1.call-start = ((), (), s32[]{:S(2)}) async-start(), calls=%async_computation.5 | async-start | bytes 1572864 | tf_op jit(solution)/shard_map/psum | solution.py:15
  253.1 56.6 %copy-start.2 = (f32[384,512]{1,0:T(8,128)S(1)}, f32[384,512]{1,0:T(8,128)}, u32[]{:S(2)}) copy-start(f32[384,512]{1,0:T(8,128)} %all-reduce.8.cloned.1.call-done) | copy-start | bytes 2359300
  255.3 54.5 %all-gather.2.cloned.1.call-start = ((), (), s32[]{:S(2)}) async-start(), calls=%async_computation.6 | async-start | bytes 2359296 | tf_op jit(solution)/shard_map/all_gather | solution.py:81
Sparse Core Ops, SparseCore 0:
  41.0 86.5 all-reduce.5
  185.8 13.3 reduce-scatter.1
  203.2 49.9 all-reduce.7
  255.4 43.8 all-reduce.9
  300.7 9.0 all-gather.1
